TPU v7x, 32 devices: a whole 2x2x4 slice. The times are simulated.
32 devices in a mesh: lat: 16 (over z, y, x), lev: 2 (over core).
Axes of the slice: x: 2, y: 2, z: 4, core: 2. Of those that a mesh axis runs over, the one named last changes fastest.
Arguments:
- grid: bfloat16 [96, 2, 48, 400], P('lat', None, 'lev'), may hold values from -6 to 6
- point_counts: int32 [96], P('lat'), may hold values from 16 to 400, as said below
- waves: int32 [96], replicated, may hold values from 0 to 95, each once
- legendre: bfloat16 [96, 96, 96], P('lat'), may hold values from -0.625 to 0.625
- weights: float32 [96], P('lat'), may hold values from 0.5 to 2
- stiffness: float32 [48], replicated, may hold values from 1e-06 to 0.0001
Outputs:
- grid_out: bfloat16 [96, 2, 48, 400], P('lat', None, 'lev')
Inputs may be any that keep to these rules, and one draw needn't show every extreme that they name: point_counts[j] is 4 j + 16 or 4 j + 20 (j counted from 0 at the pole), and the last pair has exactly 400 points. `waves`: each wavenumber from 0 to 95 appears once.
All inputs are finite; a program needn't handle non-finite values.
Results may differ from a plain program's by a relative error of at most 0.015.
Values may be sent and summed in bfloat16 or wider, within the bound.
No kernel may reach another device: no remote copies, remote signals or barrier semaphores. Data moves between devices by JAX's collectives and lax.ppermute only.
A program may use at most 128 MiB of HBM per device.

v0:
```python
import math
import jax
import jax.numpy as jnp
from jax import lax
from jax.sharding import PartitionSpec as P

TWO_PI = 2.0 * math.pi
FINE_STEPS = 32


def fourier_tables(count, wavenumbers, quarter_max):
    quarter = count // 4
    step_angle = TWO_PI / quarter.astype(jnp.float32)
    coarse_count = (quarter_max + FINE_STEPS - 1) // FINE_STEPS
    coarse_pos = FINE_STEPS * jnp.arange(coarse_count, dtype=jnp.int32)
    fine_pos = jnp.arange(FINE_STEPS, dtype=jnp.int32)
    coarse_angle = (coarse_pos[:, None] * wavenumbers[None, :] % quarter).astype(
        jnp.float32
    ) * step_angle
    fine_angle = (fine_pos[:, None] * wavenumbers[None, :] % quarter).astype(
        jnp.float32
    ) * step_angle
    coarse_cos = jnp.cos(coarse_angle)[:, None, :]
    coarse_sin = jnp.sin(coarse_angle)[:, None, :]
    fine_cos = jnp.cos(fine_angle)[None, :, :]
    fine_sin = jnp.sin(fine_angle)[None, :, :]
    full_cos = (coarse_cos * fine_cos - coarse_sin * fine_sin).reshape(
        coarse_count * FINE_STEPS, -1
    )[:quarter_max]
    full_sin = (coarse_sin * fine_cos + coarse_cos * fine_sin).reshape(
        coarse_count * FINE_STEPS, -1
    )[:quarter_max]
    positions = jnp.arange(quarter_max, dtype=jnp.int32)
    inside = (positions < quarter)[:, None]
    cosine = jnp.where(inside, full_cos, 0.0)
    sine = jnp.where(inside, full_sin, 0.0)
    matrix = jnp.concatenate([cosine, sine], axis=1).astype(jnp.bfloat16)
    offsets = jnp.arange(4, dtype=jnp.int32)
    twist = offsets[:, None] * wavenumbers[None, :] % count
    theta = twist.astype(jnp.float32) * (TWO_PI / count.astype(jnp.float32))
    return (matrix, jnp.cos(theta), jnp.sin(theta))


def helmholtz(spectra, wavenumbers, offsets, stiffness_local, width):
    full_shape = spectra.shape
    quartered = spectra.reshape(full_shape[:-2] + (full_shape[-2] // 4, 2, 2, full_shape[-1]))
    parity = (1 - 2 * (offsets % 2)).astype(jnp.float32)
    combined = quartered[..., 0, :] + parity * quartered[..., 1, :]
    degrees = (wavenumbers + offsets).astype(jnp.float32)
    inside_band = offsets < width - wavenumbers
    factor = 1.0 / (
        1.0 + stiffness_local[:, None] * degrees[..., None, :] * (degrees[..., None, :] + 1.0)
    )
    damping = jnp.where(inside_band[..., None, :], factor, 0.0)
    scaled = (combined * damping[..., :, None, :]).astype(jnp.bfloat16)
    flipped = scaled * parity.astype(jnp.bfloat16)
    return jnp.stack([scaled, flipped], axis=-2).reshape(full_shape)


def spectral(received, wavenumbers, basis, stiffness_local):
    width = basis.shape[2]
    spectra = jnp.einsum("jcr,cjl->crl", received, basis, preferred_element_type=jnp.float32)
    offsets = jnp.arange(width, dtype=jnp.int32)
    operand = helmholtz(spectra, wavenumbers[:, None], offsets, stiffness_local, width)
    returned = jnp.einsum("crl,cjl->jcr", operand, basis, preferred_element_type=jnp.float32)
    return returned.astype(jnp.bfloat16)


def on_device(grid, point_counts, waves, legendre, weights, stiffness):
    pairs, _, fields, points = grid.shape
    quarter_max = points // 4
    width = waves.shape[0]
    held_slots = legendre.shape[0]
    lat_index = lax.axis_index("lat")
    lev_index = lax.axis_index("lev")

    def analyse(pieces):
        latitude, count, weight = pieces
        matrix, twist_cos, twist_sin = fourier_tables(count, waves, quarter_max)
        values = latitude.reshape(2, fields, quarter_max, 4)
        partial_value = jnp.einsum(
            "hfab,at->hfbt", values, matrix, preferred_element_type=jnp.float32
        )
        cos_part = partial_value[..., :width]
        sin_part = partial_value[..., width:]
        real = jnp.sum(twist_cos * cos_part - twist_sin * sin_part, axis=2)
        imag = -jnp.sum(twist_sin * cos_part + twist_cos * sin_part, axis=2)
        factor = jnp.where(2 * waves < count, weight / count.astype(jnp.float32), 0.0)
        stacked = jnp.stack([real * factor, imag * factor], axis=0)
        packed = jnp.transpose(stacked, (3, 2, 0, 1)).reshape(width, 4 * fields)
        return (packed.astype(jnp.bfloat16), matrix, twist_cos, twist_sin)

    coefficients, matrices, twist_cos, twist_sin = lax.map(analyse, (grid, point_counts, weights))
    received = lax.all_to_all(coefficients, "lat", split_axis=1, concat_axis=0, tiled=True)
    owned = lax.dynamic_slice_in_dim(waves, lat_index * held_slots, held_slots)
    own_stiffness = lax.dynamic_slice_in_dim(stiffness, lev_index * fields, fields)
    synthesised = spectral(received, owned, legendre, own_stiffness)
    returned = lax.all_to_all(synthesised, "lat", split_axis=0, concat_axis=1, tiled=True)

    def synthesise(pieces):
        packed, matrix, turn_cos, turn_sin, count = pieces
        values = packed.astype(jnp.float32).reshape(width, fields, 2, 2)
        real = values[:, :, 0, :]
        imag = values[:, :, 1, :]
        factor = jnp.where(2 * waves < count, jnp.where(waves == 0, 1.0, 2.0), 0.0)[:, None, None]
        cosines = turn_cos[:, :, None, None]
        sines = turn_sin[:, :, None, None]
        turned_real = factor * (real * cosines - imag * sines)
        turned_imag = factor * (real * sines + imag * cosines)
        operand = jnp.concatenate([turned_real, -turned_imag], axis=1)
        upper = operand.astype(jnp.bfloat16)
        lower = (operand - upper.astype(jnp.float32)).astype(jnp.bfloat16)
        result = jnp.einsum("bmfh,am->hfab", upper, matrix, preferred_element_type=jnp.float32)
        result = result + jnp.einsum(
            "bmfh,am->hfab", lower, matrix, preferred_element_type=jnp.float32
        )
        return result.reshape(2, fields, points).astype(jnp.bfloat16)

    return lax.map(synthesise, (returned, matrices, twist_cos, twist_sin, point_counts))


def solution(mesh):
    in_specs = (P("lat", None, "lev", None), P("lat"), P(), P("lat", None, None), P("lat"), P())
    out_specs = P("lat", None, "lev", None)
    return jax.shard_map(
        on_device, mesh=mesh, in_specs=in_specs, out_specs=out_specs, check_vma=False
    )
```

profile of v0, /device:TPU:0, one launch (start us, length us, event | category | flops | bytes accessed | tf_op | source)
XLA Modules:
  0.0 100.6 jit_solution(9834222721202018338)
XLA Ops:
  0.0 0.7 copy-done.1
  0.7 53.4 %while.28 = (s32[]{:T(128)}, bf16[6,96,96]{1,2,0:T(8,128)(2,1)S(1)}, bf16[6,100,192]{1,2,0:T(8,128)(2,1)S(1)}, f32[6,4,96]{2,1,0:T(4,128)S(1)}, f32[6,4,96]{2,1,...) while((s32[]{:T(128)}, ...), condition=%wide.region_3.4_spmd, body=%wide.region_0.3_spmd.sunk | while | flops 7857060 | bytes 1186901 | solution.py:93
  0.7 0.6 dynamic_slice.69
  6.2 0.8 constant_dynamic-slice_fusion.4
  7.5 0.6 dynamic_slice.70
  8.8 0.6 compare_select_fusion.5
  9.6 0.6 dynamic_slice.69
  15.1 0.8 constant_dynamic-slice_fusion.4
  16.5 0.6 dynamic_slice.70
  17.7 0.6 compare_select_fusion.5
  18.5 0.6 dynamic_slice.69
  24.0 0.8 constant_dynamic-slice_fusion.4
  25.4 0.6 dynamic_slice.70
  26.6 0.6 compare_select_fusion.5
  27.4 0.6 dynamic_slice.69
  32.9 0.8 constant_dynamic-slice_fusion.4
  34.3 0.6 dynamic_slice.70
  35.5 0.6 compare_select_fusion.5
  36.3 0.6 dynamic_slice.69
  41.9 0.8 constant_dynamic-slice_fusion.4
  43.2 0.6 dynamic_slice.70
  44.4 0.6 compare_select_fusion.5
  45.2 0.6 dynamic_slice.69
  50.8 0.8 constant_dynamic-slice_fusion.4
  52.1 0.6 dynamic_slice.70
  53.3 0.6 compare_select_fusion.5
  54.1 0.8 copy.35
  55.0 8.4 %all-to-all-start = ((bf16[6,96,96]{2,0,1:T(8,128)(2,1)}), bf16[6,96,96]{2,0,1:T(8,128)(2,1)S(1)}, u32[]{:S(2)}, u32[]{:S(2)}) async-start(bf16[6,96,96]{2,0,1:T(8,128)(2,1)} %copy.35), calls=%async_computation | async-start | bytes 393216 | tf_op jit(solution)/shard_map/all_to_all | solution.py:94
  63.7 0.7 copy-done.4
  64.5 7.5 %all-to-all-done = bf16[6,96,96]{2,0,1:T(8,128)(2,1)S(1)} async-done(((bf16[6,96,96]{2,0,1:T(8,128)(2,1)}), bf16[6,96,96]{2,0,1:T(8,128)(2,1)S(1)}, u32[]{:S(2)}, u32[]{:S(2)}) %all-to-all-start) | async-done | bytes 110624 | tf_op jit(solution)/shard_map/all_to_all | solution.py:94
  72.7 0.4 pad_maximum_fusion.1
  73.3 0.8 copy.39
  74.1 3.5 %all-to-all-start.1 = ((bf16[96,6,96]{2,1,0:T(8,128)(2,1)}), bf16[96,6,96]{2,1,0:T(8,128)(2,1)S(1)}, u32[]{:S(2)}, u32[]{:S(2)}) async-start(bf16[96,6,96]{2,1,0:T(8,128)(2,1)} %copy.39), calls=%async_computation.1 | async-start | bytes 393216 | tf_op jit(solution)/shard_map/all_to_all | solution.py:98
  77.7 8.0 %all-to-all-done.1 = bf16[96,6,96]{2,1,0:T(8,128)(2,1)S(1)} async-done(((bf16[96,6,96]{2,1,0:T(8,128)(2,1)}), bf16[96,6,96]{2,1,0:T(8,128)(2,1)S(1)}, u32[]{:S(2)}, u32[]{:S(2)}) %all-to-all-start.1) | async-done | bytes 110624 | tf_op jit(solution)/shard_map/all_to_all | solution.py:98
  85.8 14.0 %while.29 = (s32[]{:T(128)}, bf16[6,2,24,400]{3,2,1,0:T(8,128)(2,1)S(1)}, bf16[6,100,192]{1,2,0:T(8,128)(2,1)S(1)}, s32[96]{0:T(128)S(1)}, s32[6]{0:T(128)S(1)},...) while((s32[]{:T(128)}, ...), condition=%wide.region_5.6_spmd, body=%wide.region_4.5_spmd.sunk | while | flops 15291362 | bytes 1428225 | solution.py:119
  86.1 0.6 dynamic_slice.75
  86.7 0.6 compare_select_fusion.6
  88.4 0.6 dynamic_slice.75
  89.0 0.6 compare_select_fusion.6
  90.8 0.6 dynamic_slice.75
  91.4 0.6 compare_select_fusion.6
  93.1 0.6 dynamic_slice.75
  93.7 0.6 compare_select_fusion.6
  95.4 0.6 dynamic_slice.75
  96.0 0.6 compare_select_fusion.6
  97.8 0.6 dynamic_slice.75
  98.4 0.6 compare_select_fusion.6
  99.9 0.7 copy-done.2
  (220 shorter events, 16.9 us)
Async XLA Ops:
  0.0 72.1 %copy-start = (bf16[6,96,96]{2,1,0:T(8,128)(2,1)S(1)}, bf16[6,96,96]{2,1,0:T(8,128)(2,1)}, u32[]{:S(2)}) copy-start(bf16[6,96,96]{2,1,0:T(8,128)(2,1)} %param.13) | copy-start | bytes 331780
  0.0 0.7 copy-start.1
  0.0 0.7 copy-start.3
  0.0 0.7 copy-start.5
  55.0 17.0 %all-to-all-start = ((bf16[6,96,96]{2,0,1:T(8,128)(2,1)}), bf16[6,96,96]{2,0,1:T(8,128)(2,1)S(1)}, u32[]{:S(2)}, u32[]{:S(2)}) async-start(bf16[6,96,96]{2,0,1:T(8,128)(2,1)} %copy.35), calls=%async_computation | async-start | bytes 393216 | tf_op jit(solution)/shard_map/all_to_all | solution.py:94
  63.7 0.7 copy-start.4
  74.1 11.6 %all-to-all-start.1 = ((bf16[96,6,96]{2,1,0:T(8,128)(2,1)}), bf16[96,6,96]{2,1,0:T(8,128)(2,1)S(1)}, u32[]{:S(2)}, u32[]{:S(2)}) async-start(bf16[96,6,96]{2,1,0:T(8,128)(2,1)} %copy.39), calls=%async_computation.1 | async-start | bytes 393216 | tf_op jit(solution)/shard_map/all_to_all | solution.py:98
  99.9 0.7 copy-start.2
where the time goes:
time: 102 us; the launch traced here: 101 us
  loops' own time  29.3 us (29%)
  local copies, waits for them, and re-layouts  24.9 us (24%)
  waiting for transfers between devices  15.5 us (15%)
  other arithmetic  14.2 us (14%)
  starting transfers between devices  11.9 us (12%)
  matrix products  4.6 us (5%)
    another operation x1, loops' own time, on_device(): lax.map(analyse, (grid, point_counts, weights))  28.8 us
    dynamic_slice x30, local copies, waits for them, and re-layouts, on_device(): lax.map(analyse, (grid, point_counts, weights))  16.5 us
    all_to_all x1, starting transfers between devices, on_device(): lax.all_to_all(coefficients, 'lat', split_axis=1, concat_axis=0, tiled=True)  8.35 us
    all_to_all x1, waiting for transfers between devices, on_device(): lax.all_to_all(synthesised, 'lat', split_axis=0, concat_axis=1, tiled=True)  8.03 us
    all_to_all x1, waiting for transfers between devices, on_device(): lax.all_to_all(coefficients, 'lat', split_axis=1, concat_axis=0, tiled=True)  7.5 us
    select_n x6, other arithmetic, synthesise(): jnp.where(2 * waves < count, jnp.where(waves == 0, 1.0, 2.0), 0.0)  3.89 us
    all_to_all x1, starting transfers between devices, on_device(): lax.all_to_all(synthesised, 'lat', split_axis=0, concat_axis=1, tiled=True)  3.52 us
    select_n x6, other arithmetic, analyse(): jnp.where(2 * waves < count, weight / count.astype(jnp.float32), 0.0)  3.37 us
  transfers between devices with their start and end apart: 2, of which 2 were waited for; matrix products, arithmetic and copies ran while one was open for 0% of the time, Pallas kernels for 0%

commit v1 on v0

--- a/solution.py
+++ b/solution.py
@@ -95,7 +95,12 @@
     owned = lax.dynamic_slice_in_dim(waves, lat_index * held_slots, held_slots)
     own_stiffness = lax.dynamic_slice_in_dim(stiffness, lev_index * fields, fields)
     synthesised = spectral(received, owned, legendre, own_stiffness)
-    returned = lax.all_to_all(synthesised, "lat", split_axis=0, concat_axis=1, tiled=True)
+    returned = jnp.concatenate(
+        lax.all_to_all(
+            jnp.stack(jnp.split(synthesised, lax.axis_size("lat"), axis=0)), "lat", 0, 0
+        ),
+        axis=1,
+    )
 
     def synthesise(pieces):
         packed, matrix, turn_cos, turn_sin, count = pieces

time: 102 us -> 110 us (1.078)
  local copies, waits for them, and re-layouts: 24.9 us -> 33.2 us
    unnamed x12 -> x27, local copies, waits for them, and re-layouts: 2.07 us -> 11.1 us
where the time goes in v1:
time: 110 us; the launch traced here: 109 us
  local copies, waits for them, and re-layouts  33.2 us (30%)
  loops' own time  29.3 us (27%)
  waiting for transfers between devices  15.5 us (14%)
  other arithmetic  14.2 us (13%)
  starting transfers between devices  11.9 us (11%)
  matrix products  4.6 us (4%)
    another operation x1, loops' own time, on_device(): lax.map(analyse, (grid, point_counts, weights))  28.8 us
    dynamic_slice x30, local copies, waits for them, and re-layouts, on_device(): lax.map(analyse, (grid, point_counts, weights))  16.5 us
    unnamed x27, local copies, waits for them, and re-layouts  11.1 us
    all_to_all x1, starting transfers between devices, on_device(): lax.all_to_all(coefficients, 'lat', split_axis=1, concat_axis=0, tiled=True)  8.35 us
    all_to_all x1, waiting for transfers between devices, on_device(): lax.all_to_all(jnp.stack(jnp.split(synthesised, lax.axis_size('lat'), axi...  8.03 us
    all_to_all x1, waiting for transfers between devices, on_device(): lax.all_to_all(coefficients, 'lat', split_axis=1, concat_axis=0, tiled=True)  7.5 us
    select_n x6, other arithmetic, synthesise(): jnp.where(2 * waves < count, jnp.where(waves == 0, 1.0, 2.0), 0.0)  3.89 us
    all_to_all x1, starting transfers between devices, on_device(): lax.all_to_all(jnp.stack(jnp.split(synthesised, lax.axis_size('lat'), axi...  3.52 us
  transfers between devices with their start and end apart: 2, of which 2 were waited for; matrix products, arithmetic and copies ran while one was open for 0% of the time, Pallas kernels for 0%

profile of v1, /device:TPU:0, one launch (start us, length us, event | category | flops | bytes accessed | tf_op | source)
XLA Modules:
  0.0 108.8 jit_solution(6132496719779512285)
XLA Ops:
  0.0 0.7 copy-done.1
  0.7 53.4 %while.28 = (s32[]{:T(128)}, bf16[6,96,96]{1,2,0:T(8,128)(2,1)S(1)}, bf16[6,100,192]{1,2,0:T(8,128)(2,1)S(1)}, f32[6,4,96]{2,1,0:T(4,128)S(1)}, f32[6,4,96]{2,1,...) while((s32[]{:T(128)}, ...), condition=%wide.region_3.4_spmd, body=%wide.region_0.3_spmd.sunk | while | flops 7857060 | bytes 1186901 | solution.py:93
  6.2 0.8 constant_dynamic-slice_fusion.4
  7.5 0.6 dynamic_slice.70
  15.1 0.8 constant_dynamic-slice_fusion.4
  16.5 0.6 dynamic_slice.70
  24.0 0.8 constant_dynamic-slice_fusion.4
  25.4 0.6 dynamic_slice.70
  33.0 0.8 constant_dynamic-slice_fusion.4
  34.3 0.6 dynamic_slice.70
  41.9 0.8 constant_dynamic-slice_fusion.4
  43.2 0.6 dynamic_slice.70
  50.8 0.8 constant_dynamic-slice_fusion.4
  52.1 0.6 dynamic_slice.70
  54.1 0.8 copy.33
  55.0 8.4 %all-to-all-start = ((bf16[6,96,96]{2,0,1:T(8,128)(2,1)}), bf16[6,96,96]{2,0,1:T(8,128)(2,1)S(1)}, u32[]{:S(2)}, u32[]{:S(2)}) async-start(bf16[6,96,96]{2,0,1:T(8,128)(2,1)} %copy.33), calls=%async_computation | async-start | bytes 393216 | tf_op jit(solution)/shard_map/all_to_all | solution.py:94
  63.7 0.7 copy-done.4
  64.5 7.5 %all-to-all-done = bf16[6,96,96]{2,0,1:T(8,128)(2,1)S(1)} async-done(((bf16[6,96,96]{2,0,1:T(8,128)(2,1)}), bf16[6,96,96]{2,0,1:T(8,128)(2,1)S(1)}, u32[]{:S(2)}, u32[]{:S(2)}) %all-to-all-start) | async-done | bytes 110624 | tf_op jit(solution)/shard_map/all_to_all | solution.py:94
  73.3 0.6 constant_dynamic-update-slice_fusion.17
  73.9 0.6 constant_dynamic-update-slice_fusion.16
  74.5 0.6 constant_dynamic-update-slice_fusion.15
  75.1 0.6 constant_dynamic-update-slice_fusion.14
  75.7 0.6 constant_dynamic-update-slice_fusion.13
  76.3 0.6 constant_dynamic-update-slice_fusion.12
  76.9 0.6 constant_dynamic-update-slice_fusion.11
  77.5 0.6 constant_dynamic-update-slice_fusion.10
  78.1 0.6 constant_dynamic-update-slice_fusion.9
  78.7 0.6 constant_dynamic-update-slice_fusion.8
  79.4 0.6 constant_dynamic-update-slice_fusion.7
  80.0 0.6 constant_dynamic-update-slice_fusion.6
  80.6 0.6 constant_dynamic-update-slice_fusion.5
  81.2 0.6 constant_dynamic-update-slice_fusion.4
  81.8 0.6 constant_dynamic-update-slice_fusion.3
  82.4 0.6 constant_dynamic-update-slice_fusion.2
  83.0 3.5 %all-to-all-start.1 = ((bf16[16,6,6,96]{3,1,2,0:T(8,128)(2,1)}), bf16[16,6,6,96]{3,1,2,0:T(8,128)(2,1)S(1)}, u32[]{:S(2)}, u32[]{:S(2)}) async-start(bf16[16,6,6,96]{3,1,2,0:T(8,128)(2,1)} %constant_dynamic-update-slice_fusion.2), calls=%async_computation.1 | async-start | bytes 393216 | tf_op jit(solution)/shard_map/all_to_all | solution.py:99
  86.5 8.0 %all-to-all-done.1 = bf16[16,6,6,96]{3,1,2,0:T(8,128)(2,1)S(1)} async-done(((bf16[16,6,6,96]{3,1,2,0:T(8,128)(2,1)}), bf16[16,6,6,96]{3,1,2,0:T(8,128)(2,1)S(1)}, u32[]{:S(2)}, u32[]{:S(2)}) %all-to-all-start.1) | async-done | bytes 110624 | tf_op jit(solution)/shard_map/all_to_all | solution.py:99
  94.7 13.4 %while.29 = (s32[]{:T(128)}, bf16[6,2,24,400]{3,2,1,0:T(8,128)(2,1)S(1)}, bf16[6,100,192]{1,2,0:T(8,128)(2,1)S(1)}, s32[96]{0:T(128)S(1)}, s32[6]{0:T(128)S(1)},...) while((s32[]{:T(128)}, ...), condition=%wide.region_5.6_spmd, body=%wide.region_4.5_spmd.sunk | while | flops 15291362 | bytes 1391361 | solution.py:124
  94.9 0.6 dynamic_slice.75
  95.5 0.6 compare_select_fusion.6
  97.1 0.6 dynamic_slice.75
  97.7 0.6 compare_select_fusion.6
  99.3 0.6 dynamic_slice.75
  99.9 0.6 compare_select_fusion.6
  101.6 0.6 dynamic_slice.75
  102.1 0.6 compare_select_fusion.6
  104.4 0.6 compare_select_fusion.6
  106.6 0.6 compare_select_fusion.6
  108.1 0.7 copy-done.2
  (228 shorter events, 24.8 us)
Async XLA Ops:
  0.0 72.1 %copy-start = (bf16[6,96,96]{2,1,0:T(8,128)(2,1)S(1)}, bf16[6,96,96]{2,1,0:T(8,128)(2,1)}, u32[]{:S(2)}) copy-start(bf16[6,96,96]{2,1,0:T(8,128)(2,1)} %param.13) | copy-start | bytes 331780
  0.0 0.7 copy-start.1
  0.0 0.7 copy-start.3
  0.0 0.7 copy-start.5
  55.0 17.0 %all-to-all-start = ((bf16[6,96,96]{2,0,1:T(8,128)(2,1)}), bf16[6,96,96]{2,0,1:T(8,128)(2,1)S(1)}, u32[]{:S(2)}, u32[]{:S(2)}) async-start(bf16[6,96,96]{2,0,1:T(8,128)(2,1)} %copy.33), calls=%async_computation | async-start | bytes 393216 | tf_op jit(solution)/shard_map/all_to_all | solution.py:94
  63.7 0.7 copy-start.4
  83.0 11.6 %all-to-all-start.1 = ((bf16[16,6,6,96]{3,1,2,0:T(8,128)(2,1)}), bf16[16,6,6,96]{3,1,2,0:T(8,128)(2,1)S(1)}, u32[]{:S(2)}, u32[]{:S(2)}) async-start(bf16[16,6,6,96]{3,1,2,0:T(8,128)(2,1)} %constant_dynamic-update-slice_fusion.2), calls=%async_computation.1 | async-start | bytes 393216 | tf_op jit(solution)/shard_map/all_to_all | solution.py:99
  108.1 0.7 copy-start.2
